TPU v7x, 256 devices: a whole 4x4x8 slice. The times are simulated.
256 devices in a mesh: ha: 32 (over z, x_hi, core), wa: 8 (over y, x_lo).
Axes of the slice: x: 4 (x_hi: 2, x_lo: 2; x = x_hi * 2 + x_lo), y: 4, z: 8, core: 2. Of those that a mesh axis runs over, the one named last changes fastest.
Arguments:
- queries: bfloat16 [512, 512, 384], P('ha', 'wa'), may hold values from -200 to 200
- key_tokens: bfloat16 [512, 512, 384], P('ha', 'wa'), may hold values from -6 to 6
- value_tokens: bfloat16 [512, 512, 384], P('ha', 'wa'), may hold values from -6 to 6
- out_grad: bfloat16 [512, 512, 384], P('ha', 'wa'), may hold values from -96 to 96
- key_kernel: bfloat16 [3, 3, 384], replicated, may hold values from -2 to 2
- value_kernel: bfloat16 [3, 3, 384], replicated, may hold values from -2 to 2
- height_table: bfloat16 [1023, 96], replicated, may hold values from -0.8984375 to 0.8984375
- width_table: bfloat16 [1023, 96], replicated, may hold values from -0.8984375 to 0.8984375
Outputs:
- query_grad: bfloat16 [512, 512, 384], P('ha', 'wa')
- key_grad: bfloat16 [512, 512, 384], P('ha', 'wa')
- value_grad: bfloat16 [512, 512, 384], P('ha', 'wa')
- height_grad: float32 [1023, 96], replicated
- width_grad: float32 [1023, 96], replicated
All inputs are finite; a program needn't handle non-finite values.
Results may differ from a plain program's by a relative error of at most 0.02.
The roundings to bfloat16 on the way count: a program that leaves them out, or rounds other values in their place, can miss the bound.
Values may be sent and summed in bfloat16 or wider, within the bound.
No kernel may reach another device: no remote copies, remote signals or barrier semaphores. Data moves between devices by JAX's collectives and lax.ppermute only.
A program may use at most 128 MiB of HBM per device.

v0:
```python
import math

import jax
import jax.numpy as jnp
from jax import lax
from jax.experimental import pallas as pl
from jax.experimental.pallas import tpu as pltpu
from jax.sharding import PartitionSpec as P

HEADS = 4
HD = 96
C = HEADS * HD
STRIDE = 16
F32 = jnp.float32
BF16 = jnp.bfloat16
SCALE = HD ** (-0.5)
ROOT = HD ** 0.5
EXPONENT = SCALE / math.log(2.0)
WIN = 256
TB = 256


def window_start(n):
    return 128 * (n // 2)


def taps(kernel, row):
    return [kernel[row, i].astype(F32) for i in range(3)]


def cell_sums(before, first, second):
    zero = jnp.zeros((1, C), F32)
    return jnp.concatenate([first + second, zero], 0) + jnp.concatenate([zero, before], 0)


def pool_partial(tokens, kernel):
    def pieces(row):
        cells = tokens[row].astype(F32).reshape(-1, STRIDE, C)
        return cells[:, STRIDE - 1], cells[:, 0], cells[:, 1]

    def weighted(row, kernel_row):
        left, mid, right = taps(kernel, kernel_row)
        before, first, second = pieces(row)
        return before * left, first * mid, second * right

    own = [a + b for a, b in zip(weighted(0, 1), weighted(1, 2))]
    return jnp.stack([cell_sums(*own), cell_sums(*weighted(STRIDE - 1, 0))])


def spread_rows(cot, kernel, kernel_row):
    left, mid, right = taps(kernel, kernel_row)
    cells = cot.shape[0] - 1
    zeros = jnp.zeros((cells, STRIDE - 3, C), F32)
    row = jnp.concatenate(
        [
            (cot[:cells] * mid)[:, None],
            (cot[:cells] * right)[:, None],
            zeros,
            (cot[1:] * left)[:, None],
        ],
        1,
    )
    return row.reshape(cells * STRIDE, C)


def spread(cot, kernel):
    top = spread_rows(cot[0], kernel, 1)
    second = spread_rows(cot[0], kernel, 2)
    last = spread_rows(cot[1], kernel, 0)
    zeros = jnp.zeros((STRIDE - 3,) + top.shape, BF16)
    return jnp.concatenate(
        [top.astype(BF16)[None], second.astype(BF16)[None], zeros, last.astype(BF16)[None]], 0
    )


def shift(block, axis, distance):
    size = lax.axis_size(axis)
    return lax.ppermute(
        block, axis, [(i, i + distance) for i in range(size) if 0 <= i + distance < size]
    )


def shift_both(block, distance):
    rows, cols = lax.axis_size("ha"), lax.axis_size("wa")
    route = [
        (i * cols + j, (i + distance) * cols + j + distance)
        for i in range(rows)
        for j in range(cols)
        if 0 <= i + distance < rows and 0 <= j + distance < cols
    ]
    return lax.ppermute(block, ("ha", "wa"), route)


def swap(block):
    return lax.ppermute(block, "ha", [(i, i ^ 1) for i in range(lax.axis_size("ha"))])


def to_all(block, axis):
    copies = jnp.broadcast_to(block[None], (lax.axis_size(axis),) + block.shape)
    return lax.all_to_all(copies, axis, 0, 0, tiled=False)


def exchange(blocks, axis):
    return lax.all_to_all(blocks, axis, 0, 0, tiled=False)


def dot(a, b):
    return jnp.dot(a, b, preferred_element_type=F32)


def token_masks(width, first):
    at = lax.broadcasted_iota(jnp.int32, (STRIDE, width), 1) + first
    entry = lax.broadcasted_iota(jnp.int32, (STRIDE, width), 0)
    return at // STRIDE == entry, at % STRIDE == entry


def prep_kernel(q_ref, g_ref, th_ref, tw_ref, qt_ref, gt_ref, hexp_ref, wexp_ref):
    jb = pl.program_id(0)
    row_mask, col_mask = token_masks(TB, 0)
    sub = lax.broadcasted_iota(jnp.int32, (8, TB), 0) % 4
    low = lax.broadcasted_iota(jnp.int32, (8, TB), 0) < 4
    qt = q_ref[...].astype(F32).reshape(TB, C).T.astype(BF16)
    gt = g_ref[...].astype(F32).reshape(TB, C).T.astype(BF16)
    shifted = pl.ds(pl.multiple_of(STRIDE * jb, STRIDE), th_ref.shape[0])
    qt_ref[...] = jnp.zeros_like(qt_ref)
    gt_ref[...] = jnp.zeros_like(gt_ref)
    for n in range(HEADS):
        left = HD * n - window_start(n)
        q_n = qt[HD * n : HD * (n + 1)]
        qt_ref[n, pl.ds(left, HD), :] = q_n
        gt_ref[n, pl.ds(left, HD), :] = gt[HD * n : HD * (n + 1)]

        def picked(table, mask):
            full = dot(table, q_n).reshape(-1, STRIDE, TB)
            full = jnp.where(mask[None], full, 0.0)
            return jnp.sum(full, axis=1, keepdims=True) * ROOT

        rel = picked(th_ref[...], row_mask)
        count = rel.shape[0]
        spread_to = lambda x: jnp.broadcast_to(x, (8, TB))
        for r in range(count // 2):
            hexp_ref[n, pl.ds(8 * r, 8), :] = jnp.where(
                low, spread_to(rel[count - 1 - 2 * r]), spread_to(rel[count - 2 - 2 * r])
            )
        rel = picked(tw_ref[shifted, :], col_mask)
        for w in range(count // 4):
            last = count - 1 - 4 * w
            value = spread_to(rel[last])
            for c in range(1, 4):
                value = jnp.where(sub == c, spread_to(rel[last - c]), value)
            wexp_ref[n, pl.ds(8 * w, 8), :] = value


def prepare(queries, out_grad, th, tw):
    rows, cols, _ = queries.shape
    tokens = rows * cols
    block = pl.BlockSpec((rows, STRIDE, C), lambda j: (0, j, 0))
    whole = lambda x: pl.BlockSpec(x.shape, lambda j: (0, 0))
    out = lambda n: pl.BlockSpec((HEADS, n, TB), lambda j: (0, 0, j))
    return pl.pallas_call(
        prep_kernel,
        grid=(tokens // TB,),
        in_specs=[block, block, whole(th), whole(tw)],
        out_specs=[out(WIN), out(WIN), out(128), out(64)],
        out_shape=[
            jax.ShapeDtypeStruct((HEADS, WIN, tokens), BF16),
            jax.ShapeDtypeStruct((HEADS, WIN, tokens), BF16),
            jax.ShapeDtypeStruct((HEADS, 128, tokens), F32),
            jax.ShapeDtypeStruct((HEADS, 64, tokens), F32),
        ],
        cost_estimate=pl.CostEstimate(
            flops=4 * 1024 * tokens * C, bytes_accessed=10 * 1024 * 1024, transcendentals=0
        ),
        name="prepare",
    )(queries, out_grad, th, tw)


def attention_kernel(
    at_ref, mine_ref, other_ref, qt_ref, gt_ref, q_ref, g_ref, hexp_ref, wexp_ref, tht_ref, twt_ref,
    keep_ref, send_ref, dq_ref,
    k_s, v_s, kt_s, vt_s, e_s, p_s, d_s, ks_s, vs_s, gh_s, gw_s, a_s, qz_s, gz_s, th_s, tw_s,
):
    n = pl.program_id(0)
    keys = k_s.shape[0]
    tokens = qt_ref.shape[2]
    groups = keys // 128
    span = tht_ref.shape[1]

    @pl.when(n == 0)
    def _():
        for parity, (k_ref, v_ref) in enumerate(
            ((mine_ref, other_ref), (other_ref, mine_ref))
        ):

            @pl.when(at_ref[2] == parity)
            def _(k_ref=k_ref, v_ref=v_ref):
                k_s[...] = k_ref[...]
                v_s[...] = v_ref[...]

        kt_s[...] = k_s[...].astype(F32).T.astype(BF16)
        vt_s[...] = v_s[...].astype(F32).T.astype(BF16)
        for ref in (ks_s, vs_s, th_s, tw_s):
            ref[...] = jnp.zeros_like(ref)

    win = pl.multiple_of(128 * (n // 2), 128)
    own = pl.multiple_of(HD * n - 128 * (n // 2), 32)
    rows = pl.multiple_of(HD * n, 32)
    kwin = pl.ds(win, WIN)
    lane = lax.broadcasted_iota(jnp.int32, (1, WIN), 1)
    lanes_on = ((lane >= own) & (lane < own + HD)).astype(F32).astype(BF16)

    for tb in range(tokens // TB):
        cols = pl.ds(tb * TB, TB)
        tile = (slice(None), pl.ds(tb * STRIDE, STRIDE), kwin)
        qz_s[cols, :] = q_ref[tile].reshape(TB, WIN) * lanes_on
        gz_s[cols, :] = g_ref[tile].reshape(TB, WIN) * lanes_on
        qt = qt_ref[0, :, cols]
        gt = gt_ref[0, :, cols]
        hexp = hexp_ref[0, :, cols]
        top = jnp.full((8, TB), -jnp.inf, F32)
        for w in range(groups):
            part = pl.ds(w * 128, 128)
            s = dot(k_s[part, kwin], qt)
            bias = wexp_ref[0, pl.ds(w * 8, 8), cols]
            s = (s + hexp).reshape(16, 8, TB) + bias[None]
            top = jnp.maximum(top, jnp.max(s, axis=0))
            e_s[part, :] = s.reshape(128, TB)
        top = jnp.max(top, axis=0, keepdims=True)
        total = jnp.zeros((8, TB), F32)
        for w in range(groups):
            part = pl.ds(w * 128, 128)
            e = jnp.exp2((e_s[part, :] - top) * EXPONENT)
            total = total + jnp.sum(e.reshape(16, 8, TB), axis=0)
            e_s[part, :] = e
        inverse = 1.0 / jnp.sum(total, axis=0, keepdims=True)
        for w in range(groups):
            part = pl.ds(w * 128, 128)
            p = e_s[part, :] * inverse
            e_s[part, :] = p
            p_s[part, cols] = p.astype(BF16)
        attended = dot(vt_s[pl.ds(rows, HD), :], p_s[:, cols])
        delta = jnp.sum(
            attended * gt_ref[0, pl.ds(own, HD), cols].astype(F32), axis=0, keepdims=True
        )
        height = jnp.zeros((128, TB), F32)
        for w in range(groups):
            part = pl.ds(w * 128, 128)
            d = e_s[part, :] * (dot(v_s[part, kwin], gt) - delta)
            d_s[part, cols] = d.astype(BF16)
            height = height + d
            width = jnp.sum(d.reshape(16, 8, TB), axis=0)
            for i in range(TB // 128):
                gw_s[i, pl.ds(w * 8, 8), :] = width[:, i * 128 : (i + 1) * 128]
        for i in range(TB // 128):
            lanes = pl.ds(tb * TB + i * 128, 128)
            row_mask, col_mask = token_masks(128, i * 128)
            gh_s[i] = height[:, i * 128 : (i + 1) * 128]
            sum_h = gh_s[i, pl.ds(0, 32, stride=4), :]
            for c in range(1, 4):
                sum_h = sum_h + gh_s[i, pl.ds(c, 32, stride=4), :]
            for k in range(32):
                a_s[pl.ds(STRIDE * (31 - k), STRIDE), lanes] = jnp.where(
                    row_mask, jnp.broadcast_to(sum_h[k : k + 1], (STRIDE, 128)), 0.0
                ).astype(BF16)
            for c in range(4):
                sum_w = (
                    gw_s[i, pl.ds(c, groups, stride=8), :] + gw_s[i, pl.ds(c + 4, groups, stride=8), :]
                )
                for w in range(groups):
                    m = 31 - 4 * w - c
                    a_s[pl.ds(span + STRIDE * m, STRIDE), lanes] = jnp.where(
                        col_mask, jnp.broadcast_to(sum_w[w : w + 1], (STRIDE, 128)), 0.0
                    ).astype(BF16)
        dq = dot(kt_s[pl.ds(rows, HD), :], d_s[:, cols]) * SCALE
        dq = dq + dot(tht_ref[...], a_s[pl.ds(0, span), cols])
        dq = dq + dot(twt_ref[tb], a_s[pl.ds(span, span), cols])
        dq_ref[0, :, cols] = dq.astype(BF16)
        tw_s[pl.ds(tb * STRIDE, span), kwin] += dot(a_s[pl.ds(span, span), cols], qz_s[cols, :])

    ks_s[:, kwin] += dot(d_s[...], qz_s[...])
    vs_s[:, kwin] += dot(p_s[...], gz_s[...])
    th_s[:, kwin] += dot(a_s[pl.ds(0, span), :], qz_s[...])

    @pl.when(n == pl.num_programs(0) - 1)
    def _():
        def heads_added(ref):
            total = ref[:, :128]
            for h in range(1, HEADS):
                first = window_start(h)
                turn = (WIN - (HD * h - first)) % WIN
                total = total + pltpu.roll(ref[:, first : first + WIN], turn, 1)[:, :128]
            return total.astype(BF16)

        def fill(k_out, v_out):
            k_out[:, pl.ds(0, C)] = (ks_s[...] * SCALE).astype(BF16)
            v_out[:, pl.ds(0, C)] = vs_s[...].astype(BF16)
            for out, ref, at in ((k_out, th_s, at_ref[0]), (v_out, tw_s, at_ref[1])):
                out[:, pl.ds(C, 128)] = jnp.zeros((keys, 128), BF16)
                first = pl.multiple_of(STRIDE * at, STRIDE)
                out[pl.ds(first, ref.shape[0]), pl.ds(C, 128)] = heads_added(ref)

        @pl.when(at_ref[2] == 0)
        def _():
            fill(keep_ref, send_ref)

        @pl.when(at_ref[2] == 1)
        def _():
            fill(send_ref, keep_ref)


def attention(at, mine, other, qt, gt, q, g, hexp, wexp, tht, twt):
    tokens = qt.shape[2]
    keys = mine.shape[0]
    span = tht.shape[1]
    whole = lambda shape: pl.BlockSpec(shape, lambda n: (0,) * len(shape))
    head = lambda shape: pl.BlockSpec((1,) + shape, lambda n: (n, 0, 0))
    return pl.pallas_call(
        attention_kernel,
        grid=(HEADS,),
        in_specs=[
            pl.BlockSpec(memory_space=pltpu.SMEM),
            whole(mine.shape),
            whole(other.shape),
            head((WIN, tokens)),
            head((WIN, tokens)),
            whole(q.shape),
            whole(g.shape),
            head((128, tokens)),
            head((64, tokens)),
            whole(tht.shape),
            whole(twt.shape),
        ],
        out_specs=[whole((keys, C + 128)), whole((keys, C + 128)), head((HD, tokens))],
        out_shape=[
            jax.ShapeDtypeStruct((keys, C + 128), BF16),
            jax.ShapeDtypeStruct((keys, C + 128), BF16),
            jax.ShapeDtypeStruct((HEADS, HD, tokens), BF16),
        ],
        scratch_shapes=[
            pltpu.VMEM((keys, C), BF16),
            pltpu.VMEM((keys, C), BF16),
            pltpu.VMEM((C, keys), BF16),
            pltpu.VMEM((C, keys), BF16),
            pltpu.VMEM((keys, TB), F32),
            pltpu.VMEM((keys, tokens), BF16),
            pltpu.VMEM((keys, tokens), BF16),
            pltpu.VMEM((keys, C), F32),
            pltpu.VMEM((keys, C), F32),
            pltpu.VMEM((TB // 128, 128, 128), F32),
            pltpu.VMEM((TB // 128, 64, 128), F32),
            pltpu.VMEM((2 * span, tokens), BF16),
            pltpu.VMEM((tokens, WIN), BF16),
            pltpu.VMEM((tokens, WIN), BF16),
            pltpu.VMEM((span, C), F32),
            pltpu.VMEM((span + STRIDE * (tokens // TB - 1), C), F32),
        ],
        compiler_params=pltpu.CompilerParams(
            dimension_semantics=("arbitrary",), vmem_limit_bytes=60 * 1024 * 1024
        ),
        cost_estimate=pl.CostEstimate(
            flops=16 * keys * tokens * C, bytes_accessed=12 * 1024 * 1024,
            transcendentals=keys * tokens * HEADS,
        ),
        name="attention",
    )(at, mine, other, qt, gt, q, g, hexp, wexp, tht, twt)


def on_device(
    queries, key_tokens, value_tokens, out_grad, key_kernel, value_kernel, height_table, width_table
):
    own_rows, own_cols, _ = queries.shape
    rows_n, cols_n = lax.axis_size("ha"), lax.axis_size("wa")
    tokens = own_rows * own_cols
    cells = own_cols // STRIDE
    ha, wa = lax.axis_index("ha"), lax.axis_index("wa")
    span = STRIDE * rows_n

    part = jnp.stack([pool_partial(key_tokens, key_kernel), pool_partial(value_tokens, value_kernel)])
    left = shift(part[:, :, cells], "wa", 1)
    part = jnp.concatenate([part[:, :, :1] + left[:, :, None], part[:, :, 1:cells]], 2)
    own = part[:, 0] + shift(part[:, 1], "ha", 1)
    pooled = own.astype(BF16)
    pooled, queries, out_grad, height_table, width_table = lax.optimization_barrier(
        (pooled, queries, out_grad, height_table, width_table)
    )
    mine = jnp.broadcast_to(pooled[None], (rows_n // 2, 2, cells, C)).reshape(rows_n, cells, C)
    mine = exchange(mine, "ha").reshape(rows_n * cells, C)
    mine = to_all(mine, "wa").reshape(cols_n * rows_n * cells, C)

    th = lax.dynamic_slice_in_dim(height_table, own_rows * ha, span, 0)
    tw = lax.dynamic_slice_in_dim(width_table, own_cols * wa, span + STRIDE * (cells - 1), 0)
    tht = th.T
    twt = jnp.stack([tw[STRIDE * a : STRIDE * a + span].T for a in range(cells)])
    qt, gt, hexp, wexp = prepare(queries, out_grad, th, tw)
    mine, tht, twt, qt, gt, hexp, wexp = lax.optimization_barrier(
        (mine, tht, twt, qt, gt, hexp, wexp)
    )
    other = swap(mine)

    at = jnp.stack([ha, wa * cells, ha % 2]).astype(jnp.int32)
    keep, send, dq = attention(
        at, mine, other, qt, gt, queries, out_grad, hexp, wexp, tht, twt
    )

    sums = (keep.astype(F32) + swap(send).astype(F32)).astype(BF16)
    sums = exchange(sums.reshape(cols_n, rows_n * cells, C + 128), "wa")
    sums = jnp.sum(sums.astype(F32), 0).astype(BF16)
    half = rows_n * cells // 2
    table = sums[:, C : C + HD].reshape(1, 2, cells, half // cells * HD)
    table = jnp.broadcast_to(table, (rows_n // 2,) + table.shape[1:])
    sums = jnp.concatenate(
        [sums[:, :C].reshape(rows_n, cells, C), table.reshape(rows_n, cells, half // cells * HD)], 2
    )
    sums = exchange(sums, "ha")
    sums = jnp.sum(sums.reshape(rows_n // 2, 2, cells, -1).astype(F32), 0)
    table = sums[:, :, C:].astype(BF16).reshape(2, half, HD)
    table = jnp.pad(table, ((0, 0), (0, 0), (0, 128 - HD)))
    table = to_all(jnp.concatenate([table[0], table[1]], 1), "wa")
    far = swap(table)
    table = jnp.stack([jnp.where(ha % 2 == 0, table, far), jnp.where(ha % 2 == 0, far, table)], 1)
    table = table.reshape(2 * span, 256)
    height_grad = table[: height_table.shape[0], :HD].astype(F32)
    width_grad = table[: width_table.shape[0], 128 : 128 + HD].astype(F32)
    sums = sums[:, :, :C]

    right = shift(sums[:, :1], "wa", -1)
    below = shift(sums, "ha", -1)
    corner = shift_both(sums[:, :1], -1)
    cot = jnp.stack(
        [jnp.concatenate([sums, right], 1), jnp.concatenate([below, corner], 1)], 1
    )
    key_grad = spread(cot[0], key_kernel)
    value_grad = spread(cot[1], value_kernel)

    query_grad = dq.reshape(C, cells, own_rows, STRIDE).transpose(2, 1, 3, 0)
    query_grad = query_grad.reshape(own_rows, own_cols, C)
    return (query_grad, key_grad, value_grad, height_grad, width_grad)


def solution(mesh):
    placed = P("ha", "wa", None)
    return jax.shard_map(
        on_device,
        mesh=mesh,
        in_specs=(placed,) * 4 + (P(),) * 4,
        out_specs=(placed, placed, placed, P(), P()),
        check_vma=False,
    )
```

profile of v0, /device:TPU:2, one launch (start us, length us, event | category | flops | bytes accessed | tf_op | source)
XLA Modules:
  0.0 161.7 jit_solution(900334999078566870)
XLA Ops:
  0.6 0.9 convert_reduce_fusion.18
  1.5 0.9 fusion.46
  2.5 0.9 convert_reduce_fusion.9
  3.4 0.9 fusion.47
  4.5 3.5 %collective-permute-start = (f32[2,2,384]{2,1,0:T(2,128)S(1)}, f32[2,2,384]{2,1,0:T(2,128)S(1)}, u32[]{:S(2)}, u32[]{:S(2)}) collective-permute-start(f32[2,2,384]{2,1,0:T(2,128)S(1)} %bitcast.281), channel_id=1, source_target_pairs={{0,1},{1,2},{2,3},{3,4},{4,5},{5,6},{6,7},{8,9},{9,10},{10,11},{11... | collective-permute-start | bytes 18440 | tf_op jit(solution)/shard_map/ppermute | solution.py:78
  8.0 2.1 %collective-permute-done = f32[2,2,384]{2,1,0:T(2,128)S(1)} collective-permute-done((f32[2,2,384]{2,1,0:T(2,128)S(1)}, f32[2,2,384]{2,1,0:T(2,128)S(1)}, u32[]{:S(2)}, u32[]{:S(2)}) %collective-permute-start) | collective-permute-done | bytes 6176 | tf_op jit(solution)/shard_map/ppermute | solution.py:78
  10.1 1.3 collective-permute-start.1
  11.4 0.8 collective-permute-done.1
  12.2 0.7 broadcast_in_dim.15
  12.9 15.4 %all-to-all-start = ((bf16[32,4,384]{2,1,0:T(4,128)(2,1)}), bf16[32,4,384]{2,1,0:T(4,128)(2,1)S(1)}, u32[]{:S(2)}, u32[]{:S(2)}) async-start(bf16[32,4,384]{2,1,0:T(4,128)(2,1)} %bitcast.36), calls=%async_computation | async-start | bytes 196608 | tf_op jit(solution)/shard_map/all_to_all | solution.py:104
  28.3 10.2 %all-to-all-done = bf16[32,4,384]{2,1,0:T(4,128)(2,1)S(1)} async-done(((bf16[32,4,384]{2,1,0:T(4,128)(2,1)}), bf16[32,4,384]{2,1,0:T(4,128)(2,1)S(1)}, u32[]{:S(2)}, u32[]{:S(2)}) %all-to-all-start) | async-done | bytes 98336 | tf_op jit(solution)/shard_map/all_to_all | solution.py:104
  38.5 1.0 broadcast_in_dim.17
  39.4 6.2 %all-to-all-start.1 = ((bf16[8,128,384]{2,1,0:T(8,128)(2,1)}), bf16[8,128,384]{2,1,0:T(8,128)(2,1)S(1)}, u32[]{:S(2)}, u32[]{:S(2)}) async-start(bf16[8,128,384]{2,1,0:T(8,128)(2,1)} %broadcast_in_dim.17), calls=%async_computation.1 | async-start | bytes 1572864 | tf_op jit(solution)/shard_map/all_to_all | solution.py:100
  45.8 0.8 copy.187.tw_ref
  46.7 0.8 copy.186.th_ref
  47.5 0.7 fusion.54.tht_ref
  48.2 0.2 dynamic-slice_bitcast_fusion.3
  48.4 0.8 pad_maximum_fusion.4.twt_ref
  49.2 7.1 %prepare.1 = (bf16[4,256,1024]{2,1,0:T(8,128)(2,1)}, bf16[4,256,1024]{2,1,0:T(8,128)(2,1)}, f32[4,128,1024]{2,1,0:T(8,128)}, f32[4,64,1024]{2,1,0:T(8,128)}) custom-call(bf16[16,64,384]{2,1,0:T(8,128)(2,1)} %q_ref.1, bf16[16,64,384]{2,1,0:T(8,128)(2,1)} %g_ref.1, bf16[512,96]{1,0:T(8,128)(2,1)} %copy.186.th_ref, bf16[560,96]{1,0:T(8,128)(2,1)} %copy.187.tw_ref), custom_call_target="tpu_custom_call" | custom-call | flops 1610612736 | bytes 10485760 | tf_op jit(solution)/shard_map/prepare/pallas_call | solution.py:160
  56.2 1.7 %all-to-all-done.1 = bf16[8,128,384]{2,1,0:T(8,128)(2,1)S(1)} async-done(((bf16[8,128,384]{2,1,0:T(8,128)(2,1)}), bf16[8,128,384]{2,1,0:T(8,128)(2,1)S(1)}, u32[]{:S(2)}, u32[]{:S(2)}) %all-to-all-start.1) | async-done | bytes 786464 | tf_op jit(solution)/shard_map/all_to_all | solution.py:100
  57.9 0.7 pad_add_fusion.at_ref
  58.7 1.6 collective-permute-done.2.other_ref
  60.2 0.9 copy-done.4
  61.1 32.8 %attention.1 = (bf16[1024,512]{1,0:T(8,128)(2,1)}, bf16[1024,512]{1,0:T(8,128)(2,1)}, bf16[4,96,1024]{2,1,0:T(8,128)(2,1)}) custom-call(s32[3]{0:T(128)} %pad_add_fusion.at_ref, bf16[1024,384]{1,0:T(8,128)(2,1)} %bitcast.268, bf16[1024,384]{1,0:T(8,128)(2,1)} %copy-done.4, bf16[4,256,1024]{2,1,0:T(8,128)(2,1)} %get-tuple-element.34.qt_ref, ...), custom_call_target="tpu_custom_call" | custom-call | flops 6442450944 | bytes 12582912 | tf_op jit(solution)/shard_map/attention/pallas_call | solution.py:317
  93.9 0.2 collective-permute-start.3
  94.2 2.7 %collective-permute-done.3 = bf16[1024,512]{1,0:T(8,128)(2,1)S(1)} collective-permute-done((bf16[1024,512]{1,0:T(8,128)(2,1)}, bf16[1024,512]{1,0:T(8,128)(2,1)S(1)}, u32[]{:S(2)}, u32[]{:S(2)}) %collective-permute-start.3) | collective-permute-done | bytes 1048608 | tf_op jit(solution)/shard_map/ppermute | solution.py:95
  96.9 1.5 add_convert_fusion
  98.4 18.9 %all_to_all.25 = bf16[8,128,512]{2,1,0:T(8,128)(2,1)S(1)} all-to-all(bf16[8,128,512]{2,1,0:T(8,128)(2,1)S(1)} %bitcast.261), channel_id=1, replica_groups=mesh['ha'=32,'wa'=8] {'wa'}, dimensions={0} | all-to-all | bytes 2097152 | tf_op jit(solution)/shard_map/all_to_all | solution.py:104
  117.4 0.1 reduce_sum.21
  117.8 1.0 pad_maximum_fusion.3
  118.8 4.1 %all-to-all-start.3 = ((bf16[32,4,1920]{2,1,0:T(4,128)(2,1)}), bf16[32,4,1920]{2,1,0:T(4,128)(2,1)S(1)}, u32[]{:S(2)}, u32[]{:S(2)}) async-start(bf16[32,4,1920]{2,1,0:T(4,128)(2,1)} %pad_maximum_fusion.3), calls=%async_computation.3 | async-start | bytes 983040 | tf_op jit(solution)/shard_map/all_to_all | solution.py:104
  123.0 0.7 copy.188
  123.8 0.7 reshape.793
  124.4 1.0 copy.189
  125.5 14.6 %all-to-all-done.3 = bf16[32,4,1920]{2,1,0:T(4,128)(2,1)S(1)} async-done(((bf16[32,4,1920]{2,1,0:T(4,128)(2,1)}), bf16[32,4,1920]{2,1,0:T(4,128)(2,1)S(1)}, u32[]{:S(2)}, u32[]{:S(2)}) %all-to-all-start.3) | async-done | bytes 491552 | tf_op jit(solution)/shard_map/all_to_all | solution.py:104
  140.0 0.2 convert_reduce_fusion
  140.2 1.3 collective-permute-start.6
  141.5 3.1 %collective-permute-start.4 = (f32[2,1,384]{2,1,0:T(1,128)S(1)}, f32[2,1,384]{2,1,0:T(1,128)S(1)}, u32[]{:S(2)}, u32[]{:S(2)}) collective-permute-start(f32[2,1,384]{2,1,0:T(1,128)S(1)} %slice.414), channel_id=1, source_target_pairs={{1,0},{2,1},{3,2},{4,3},{5,4},{6,5},{7,6},{9,8},{10,9},{11,10},{12... | collective-permute-start | bytes 9224 | tf_op jit(solution)/shard_map/ppermute | solution.py:78
  144.8 0.7 broadcast_in_dim.20
  145.5 4.2 %all-to-all-start.4 = ((bf16[8,64,256]{2,1,0:T(8,128)(2,1)}), bf16[8,64,256]{2,1,0:T(8,128)(2,1)S(1)}, u32[]{:S(2)}, u32[]{:S(2)}) async-start(bf16[8,64,256]{2,1,0:T(8,128)(2,1)} %broadcast_in_dim.20), calls=%async_computation.4 | async-start | bytes 524288 | tf_op jit(solution)/shard_map/all_to_all | solution.py:100
  149.7 1.3 collective-permute-start.5
  151.3 2.3 %collective-permute-done.5 = f32[2,4,384]{2,1,0:T(4,128)S(1)} collective-permute-done((f32[2,4,384]{2,1,0:T(4,128)S(1)}, f32[2,4,384]{2,1,0:T(4,128)S(1)}, u32[]{:S(2)}, u32[]{:S(2)}) %collective-permute-start.5) | collective-permute-done | bytes 12320 | tf_op jit(solution)/shard_map/ppermute | solution.py:78
  153.8 0.2 pad_maximum_fusion.8
  154.0 2.4 %all-to-all-done.4 = bf16[8,64,256]{2,1,0:T(8,128)(2,1)S(1)} async-done(((bf16[8,64,256]{2,1,0:T(8,128)(2,1)}), bf16[8,64,256]{2,1,0:T(8,128)(2,1)S(1)}, u32[]{:S(2)}, u32[]{:S(2)}) %all-to-all-start.4) | async-done | bytes 262176 | tf_op jit(solution)/shard_map/all_to_all | solution.py:100
  156.3 1.9 %collective-permute-start.7 = (bf16[8,64,256]{2,1,0:T(8,128)(2,1)S(1)}, bf16[8,64,256]{2,1,0:T(8,128)(2,1)S(1)}, u32[]{:S(2)}, u32[]{:S(2)}) collective-permute-start(bf16[8,64,256]{2,1,0:T(8,128)(2,1)S(1)} %all-to-all-done.4), channel_id=1, source_target_pairs={{0,8},{8,0},{16,24},{24,16},{32,40},{40,32},{48,56},{56,48},{64,72... | collective-permute-start | bytes 786440 | tf_op jit(solution)/shard_map/ppermute | solution.py:95
  158.2 1.3 pad_maximum_fusion.1
  159.8 0.9 copy.210
  160.8 0.9 copy.211
  (83 shorter events, 1.4 us)
Async XLA Ops:
  0.6 46.0 %copy-start = (bf16[1023,96]{0,1:T(8,128)(2,1)S(1)}, bf16[1023,96]{0,1:T(8,128)(2,1)}, u32[]{:S(2)}) copy-start(bf16[1023,96]{0,1:T(8,128)(2,1)} %param.14) | copy-start | bytes 589252
  2.5 43.2 %copy-start.1 = (bf16[1023,96]{0,1:T(8,128)(2,1)S(1)}, bf16[1023,96]{0,1:T(8,128)(2,1)}, u32[]{:S(2)}) copy-start(bf16[1023,96]{0,1:T(8,128)(2,1)} %param.15) | copy-start | bytes 589252
  4.5 5.5 %collective-permute-start = (f32[2,2,384]{2,1,0:T(2,128)S(1)}, f32[2,2,384]{2,1,0:T(2,128)S(1)}, u32[]{:S(2)}, u32[]{:S(2)}) collective-permute-start(f32[2,2,384]{2,1,0:T(2,128)S(1)} %bitcast.281), channel_id=1, source_target_pairs={{0,1},{1,2},{2,3},{3,4},{4,5},{5,6},{6,7},{8,9},{9,10},{10,11},{11... | collective-permute-start | bytes 18440 | tf_op jit(solution)/shard_map/ppermute | solution.py:78
  10.1 2.1 %collective-permute-start.1 = (f32[2,4,384]{2,1,0:T(4,128)S(1)}, f32[2,4,384]{2,1,0:T(4,128)S(1)}, u32[]{:S(2)}, u32[]{:S(2)}) collective-permute-start(f32[2,4,384]{2,1,0:T(4,128)S(1)} %slice_bitcast_fusion), channel_id=1, source_target_pairs={{0,8},{8,16},{16,24},{24,32},{32,40},{40,48},{48,56},{56,64},{64,7... | collective-permute-start | bytes 36872 | tf_op jit(solution)/shard_map/ppermute | solution.py:78
  12.9 25.6 %all-to-all-start = ((bf16[32,4,384]{2,1,0:T(4,128)(2,1)}), bf16[32,4,384]{2,1,0:T(4,128)(2,1)S(1)}, u32[]{:S(2)}, u32[]{:S(2)}) async-start(bf16[32,4,384]{2,1,0:T(4,128)(2,1)} %bitcast.36), calls=%async_computation | async-start | bytes 196608 | tf_op jit(solution)/shard_map/all_to_all | solution.py:104
  39.4 18.5 %all-to-all-start.1 = ((bf16[8,128,384]{2,1,0:T(8,128)(2,1)}), bf16[8,128,384]{2,1,0:T(8,128)(2,1)S(1)}, u32[]{:S(2)}, u32[]{:S(2)}) async-start(bf16[8,128,384]{2,1,0:T(8,128)(2,1)} %broadcast_in_dim.17), calls=%async_computation.1 | async-start | bytes 1572864 | tf_op jit(solution)/shard_map/all_to_all | solution.py:100
  57.9 2.3 %copy-start.3 = (bf16[8,128,384]{2,1,0:T(8,128)(2,1)}, bf16[8,128,384]{2,1,0:T(8,128)(2,1)S(1)}, u32[]{:S(2)}) copy-start(bf16[8,128,384]{2,1,0:T(8,128)(2,1)S(1)} %all-to-all-done.1) | copy-start | bytes 2359300
  57.9 2.3 %collective-permute-start.2 = (bf16[1024,384]{1,0:T(8,128)(2,1)S(1)}, bf16[1024,384]{1,0:T(8,128)(2,1)S(1)}, u32[]{:S(2)}, u32[]{:S(2)}) collective-permute-start(bf16[1024,384]{1,0:T(8,128)(2,1)S(1)} %bitcast.267), channel_id=1, source_target_pairs={{0,8},{8,0},{16,24},{24,16},{32,40},{40,32},{48,56},{56,48},{64,72... | collective-permute-start | bytes 2359304 | tf_op jit(solution)/shard_map/ppermute | solution.py:95
  60.2 0.9 copy-start.4
  93.9 3.0 %collective-permute-start.3 = (bf16[1024,512]{1,0:T(8,128)(2,1)}, bf16[1024,512]{1,0:T(8,128)(2,1)S(1)}, u32[]{:S(2)}, u32[]{:S(2)}) collective-permute-start(bf16[1024,512]{1,0:T(8,128)(2,1)} %get-tuple-element.42), channel_id=1, source_target_pairs={{0,8},{8,0},{16,24},{24,16},{32,40},{40,32},{48,56},{56,48},{64,72... | collective-permute-start | bytes 3145736 | tf_op jit(solution)/shard_map/ppermute | solution.py:95
  117.4 5.7 %copy-start.2 = (bf16[4,96,1024]{2,1,0:T(8,128)(2,1)S(1)}, bf16[4,96,1024]{2,1,0:T(8,128)(2,1)}, u32[]{:S(2)}) copy-start(bf16[4,96,1024]{2,1,0:T(8,128)(2,1)} %get-tuple-element.40) | copy-start | bytes 2359300
  118.8 21.2 %all-to-all-start.3 = ((bf16[32,4,1920]{2,1,0:T(4,128)(2,1)}), bf16[32,4,1920]{2,1,0:T(4,128)(2,1)S(1)}, u32[]{:S(2)}, u32[]{:S(2)}) async-start(bf16[32,4,1920]{2,1,0:T(4,128)(2,1)} %pad_maximum_fusion.3), calls=%async_computation.3 | async-start | bytes 983040 | tf_op jit(solution)/shard_map/all_to_all | solution.py:104
  140.2 11.0 %collective-permute-start.6 = (f32[2,1,384]{2,1,0:T(1,128)S(1)}, f32[2,1,384]{2,1,0:T(1,128)S(1)}, u32[]{:S(2)}, u32[]{:S(2)}) collective-permute-start(f32[2,1,384]{2,1,0:T(1,128)S(1)} %slice.414), channel_id=1, source_target_pairs={{9,0},{10,1},{11,2},{12,3},{13,4},{14,5},{15,6},{17,8},{18,9},{19,... | collective-permute-start | bytes 9224 | tf_op jit(solution)/shard_map/ppermute | solution.py:91
  141.5 9.4 %collective-permute-start.4 = (f32[2,1,384]{2,1,0:T(1,128)S(1)}, f32[2,1,384]{2,1,0:T(1,128)S(1)}, u32[]{:S(2)}, u32[]{:S(2)}) collective-permute-start(f32[2,1,384]{2,1,0:T(1,128)S(1)} %slice.414), channel_id=1, source_target_pairs={{1,0},{2,1},{3,2},{4,3},{5,4},{6,5},{7,6},{9,8},{10,9},{11,10},{12... | collective-permute-start | bytes 9224 | tf_op jit(solution)/shard_map/ppermute | solution.py:78
  145.5 10.9 %all-to-all-start.4 = ((bf16[8,64,256]{2,1,0:T(8,128)(2,1)}), bf16[8,64,256]{2,1,0:T(8,128)(2,1)S(1)}, u32[]{:S(2)}, u32[]{:S(2)}) async-start(bf16[8,64,256]{2,1,0:T(8,128)(2,1)} %broadcast_in_dim.20), calls=%async_computation.4 | async-start | bytes 524288 | tf_op jit(solution)/shard_map/all_to_all | solution.py:100
  149.7 3.9 %collective-permute-start.5 = (f32[2,4,384]{2,1,0:T(4,128)S(1)}, f32[2,4,384]{2,1,0:T(4,128)S(1)}, u32[]{:S(2)}, u32[]{:S(2)}) collective-permute-start(f32[2,4,384]{2,1,0:T(4,128)S(1)} %slice.413), channel_id=1, source_target_pairs={{8,0},{16,8},{24,16},{32,24},{40,32},{48,40},{56,48},{64,56},{72,6... | collective-permute-start | bytes 36872 | tf_op jit(solution)/shard_map/ppermute | solution.py:78
  156.3 3.2 %collective-permute-start.7 = (bf16[8,64,256]{2,1,0:T(8,128)(2,1)S(1)}, bf16[8,64,256]{2,1,0:T(8,128)(2,1)S(1)}, u32[]{:S(2)}, u32[]{:S(2)}) collective-permute-start(bf16[8,64,256]{2,1,0:T(8,128)(2,1)S(1)} %all-to-all-done.4), channel_id=1, source_target_pairs={{0,8},{8,0},{16,24},{24,16},{32,40},{40,32},{48,56},{56,48},{64,72... | collective-permute-start | bytes 786440 | tf_op jit(solution)/shard_map/ppermute | solution.py:95
where the time goes:
time: 164 us; the launch traced here: 162 us
  starting transfers between devices  42.4 us (26%)
  Pallas kernels  39.9 us (24%)
  waiting for transfers between devices  38.3 us (23%)
  blocking collectives  18.9 us (12%)
  local copies, waits for them, and re-layouts  12.7 us (8%)
  other arithmetic  8.16 us (5%)
    pallas_call x1, Pallas kernels, attention(): pl.pallas_call(attention_kernel, grid=(HEADS,), in_specs=[pl.BlockSpec(me...  32.8 us
    all_to_all x2, waiting for transfers between devices, exchange(): return lax.all_to_all(blocks, axis, 0, 0, tiled=False)  24.7 us
    all_to_all x2, starting transfers between devices, exchange(): return lax.all_to_all(blocks, axis, 0, 0, tiled=False)  19.5 us
    all_to_all x1, blocking collectives, exchange(): return lax.all_to_all(blocks, axis, 0, 0, tiled=False)  18.9 us
    all_to_all x2, starting transfers between devices, to_all(): return lax.all_to_all(copies, axis, 0, 0, tiled=False)  10.4 us
    ppermute x4, starting transfers between devices, shift(): lax.ppermute(block, axis, [(i, i + distance) for i in range(size) if 0 <=...  9.1 us
    pallas_call x1, Pallas kernels, prepare(): pl.pallas_call(prep_kernel, grid=(tokens // TB,), in_specs=[block, block,...  7.05 us
    ppermute x4, waiting for transfers between devices, shift(): lax.ppermute(block, axis, [(i, i + distance) for i in range(size) if 0 <=...  5.22 us
  transfers between devices with their start and end apart: 12, of which 9 were waited for; matrix products, arithmetic and copies ran while one was open for 6% of the time, Pallas kernels for 4%

commit v1 on v0

--- a/solution.py
+++ b/solution.py
@@ -6,6 +6,7 @@
 from jax.experimental import pallas as pl
 from jax.experimental.pallas import tpu as pltpu
 from jax.sharding import PartitionSpec as P
+
 
 HEADS = 4
 HD = 96
@@ -24,53 +25,94 @@
     return 128 * (n // 2)
 
 
-def taps(kernel, row):
-    return [kernel[row, i].astype(F32) for i in range(3)]
-
-
-def cell_sums(before, first, second):
-    zero = jnp.zeros((1, C), F32)
-    return jnp.concatenate([first + second, zero], 0) + jnp.concatenate([zero, before], 0)
-
-
-def pool_partial(tokens, kernel):
-    def pieces(row):
-        cells = tokens[row].astype(F32).reshape(-1, STRIDE, C)
-        return cells[:, STRIDE - 1], cells[:, 0], cells[:, 1]
-
-    def weighted(row, kernel_row):
-        left, mid, right = taps(kernel, kernel_row)
-        before, first, second = pieces(row)
-        return before * left, first * mid, second * right
-
-    own = [a + b for a, b in zip(weighted(0, 1), weighted(1, 2))]
-    return jnp.stack([cell_sums(*own), cell_sums(*weighted(STRIDE - 1, 0))])
-
-
-def spread_rows(cot, kernel, kernel_row):
-    left, mid, right = taps(kernel, kernel_row)
-    cells = cot.shape[0] - 1
-    zeros = jnp.zeros((cells, STRIDE - 3, C), F32)
-    row = jnp.concatenate(
-        [
-            (cot[:cells] * mid)[:, None],
-            (cot[:cells] * right)[:, None],
-            zeros,
-            (cot[1:] * left)[:, None],
-        ],
-        1,
-    )
-    return row.reshape(cells * STRIDE, C)
-
-
-def spread(cot, kernel):
-    top = spread_rows(cot[0], kernel, 1)
-    second = spread_rows(cot[0], kernel, 2)
-    last = spread_rows(cot[1], kernel, 0)
-    zeros = jnp.zeros((STRIDE - 3,) + top.shape, BF16)
-    return jnp.concatenate(
-        [top.astype(BF16)[None], second.astype(BF16)[None], zeros, last.astype(BF16)[None]], 0
-    )
+def pool_kernel(k0, k1, k15, v0, v1, v15, kk_ref, vk_ref, own_ref, down_ref, right_ref, corner_ref):
+    cells = own_ref.shape[1]
+    for t, (rows, kernel) in enumerate((((k0, k1, k15), kk_ref), ((v0, v1, v15), vk_ref))):
+        weight = [kernel[i].astype(F32) for i in range(3)]
+        tap = lambda i, j: weight[i][j : j + 1]
+        own, down = [0.0] * (cells + 1), [0.0] * (cells + 1)
+        for c in range(cells):
+            top, second, last = [
+                x[0, pl.ds(STRIDE * c, STRIDE), :].astype(F32) for x in rows
+            ]
+            for i, x, to in ((1, top, own), (2, second, own), (0, last, down)):
+                to[c] = to[c] + (x[0:1] * tap(i, 1) + x[1:2] * tap(i, 2))
+                to[c + 1] = to[c + 1] + x[STRIDE - 1 : STRIDE] * tap(i, 0)
+        for c in range(cells):
+            own_ref[t, pl.ds(c, 1), :] = own[c]
+            down_ref[t, pl.ds(c, 1), :] = down[c]
+        right_ref[t] = own[cells]
+        corner_ref[t] = down[cells]
+
+
+def pool_partial(key_tokens, value_tokens, key_kernel, value_kernel):
+    _, cols, _ = key_tokens.shape
+    cells = cols // STRIDE
+    row = lambda r: pl.BlockSpec((1, cols, C), lambda i, r=r: (r, 0, 0))
+    whole = lambda shape: pl.BlockSpec(shape, lambda i: (0,) * len(shape))
+    rows = [row(0), row(1), row(STRIDE - 1)]
+    shapes = [(2, cells, C), (2, cells, C), (2, 1, C), (2, 1, C)]
+    return pl.pallas_call(
+        pool_kernel,
+        grid=(1,),
+        in_specs=rows + rows + [whole(key_kernel.shape), whole(value_kernel.shape)],
+        out_specs=[whole(x) for x in shapes],
+        out_shape=[jax.ShapeDtypeStruct(x, F32) for x in shapes],
+        name="pool",
+    )(*(key_tokens,) * 3, *(value_tokens,) * 3, key_kernel, value_kernel)
+
+
+def pooled_kernel(own_ref, above_ref, left_ref, corner_ref, out_ref):
+    for t in range(2):
+        full = own_ref[t] + above_ref[t]
+        first = full[0:1] + (left_ref[t] + corner_ref[t])
+        at = lax.broadcasted_iota(jnp.int32, full.shape, 0)
+        full = jnp.where(at == 0, jnp.broadcast_to(first, full.shape), full).astype(BF16)
+        for i in range(out_ref.shape[0] // 2):
+            out_ref[2 * i + t] = full
+
+
+def pooled_copies(own, above, left, corner, copies):
+    whole = pl.BlockSpec(memory_space=pltpu.VMEM)
+    return pl.pallas_call(
+        pooled_kernel,
+        in_specs=[whole] * 4,
+        out_specs=whole,
+        out_shape=jax.ShapeDtypeStruct((copies,) + own.shape[1:], BF16),
+        name="pooled",
+    )(own, above, left, corner)
+
+
+def spread_kernel(
+    sums_ref, right_ref, below_ref, corner_ref, kk_ref, vk_ref, key_out_ref, value_out_ref
+):
+    cells = sums_ref.shape[1]
+    at = lax.broadcasted_iota(jnp.int32, (STRIDE, C), 0)
+    wide = lambda x: jnp.broadcast_to(x, (STRIDE, C))
+    for t, (kernel, out) in enumerate(((kk_ref, key_out_ref), (vk_ref, value_out_ref))):
+        weight = [kernel[i].astype(F32) for i in range(3)]
+        tap = lambda i, j: weight[i][j : j + 1]
+        own, low = sums_ref[t], below_ref[t]
+        near = [own[c : c + 1] for c in range(cells)] + [right_ref[t]]
+        far = [low[c : c + 1] for c in range(cells)] + [corner_ref[t]]
+        out[...] = jnp.zeros_like(out)
+        for row, i, cell in ((0, 1, near), (1, 2, near), (STRIDE - 1, 0, far)):
+            for c in range(cells):
+                value = jnp.where(at == 0, wide(cell[c] * tap(i, 1)), 0.0)
+                value = jnp.where(at == 1, wide(cell[c] * tap(i, 2)), value)
+                value = jnp.where(at == STRIDE - 1, wide(cell[c + 1] * tap(i, 0)), value)
+                out[row, pl.ds(STRIDE * c, STRIDE), :] = value.astype(BF16)
+
+
+def spread(sums, right, below, corner, key_kernel, value_kernel, shape):
+    whole = pl.BlockSpec(memory_space=pltpu.VMEM)
+    return pl.pallas_call(
+        spread_kernel,
+        in_specs=[whole] * 6,
+        out_specs=[whole] * 2,
+        out_shape=[jax.ShapeDtypeStruct(shape, BF16)] * 2,
+        name="spread",
+    )(sums, right, below, corner, key_kernel, value_kernel)
 
 
 def shift(block, axis, distance):
@@ -209,35 +251,43 @@
     lane = lax.broadcasted_iota(jnp.int32, (1, WIN), 1)
     lanes_on = ((lane >= own) & (lane < own + HD)).astype(F32).astype(BF16)
 
-    for tb in range(tokens // TB):
+    blocks = tokens // TB
+    for tb in range(blocks):
+        tile = (slice(None), pl.ds(tb * STRIDE, STRIDE), kwin)
+        qz_s[pl.ds(tb * TB, TB), :] = q_ref[tile].reshape(TB, WIN) * lanes_on
+        gz_s[pl.ds(tb * TB, TB), :] = g_ref[tile].reshape(TB, WIN) * lanes_on
+
+    def scores(tb, w, top):
+        cols, part = pl.ds(tb * TB, TB), pl.ds(w * 128, 128)
+        s = dot(k_s[part, kwin], qt_ref[0, :, cols])
+        bias = wexp_ref[0, pl.ds(w * 8, 8), cols]
+        s = (s + hexp_ref[0, :, cols]).reshape(16, 8, TB) + bias[None]
+        e_s[tb % 2, part, :] = s.reshape(128, TB)
+        return jnp.maximum(top, jnp.max(s, axis=0))
+
+    lowest = jnp.full((8, TB), -jnp.inf, F32)
+    following = lowest
+    for w in range(groups):
+        following = scores(0, w, following)
+    for tb in range(blocks):
         cols = pl.ds(tb * TB, TB)
-        tile = (slice(None), pl.ds(tb * STRIDE, STRIDE), kwin)
-        qz_s[cols, :] = q_ref[tile].reshape(TB, WIN) * lanes_on
-        gz_s[cols, :] = g_ref[tile].reshape(TB, WIN) * lanes_on
-        qt = qt_ref[0, :, cols]
-        gt = gt_ref[0, :, cols]
-        hexp = hexp_ref[0, :, cols]
-        top = jnp.full((8, TB), -jnp.inf, F32)
-        for w in range(groups):
-            part = pl.ds(w * 128, 128)
-            s = dot(k_s[part, kwin], qt)
-            bias = wexp_ref[0, pl.ds(w * 8, 8), cols]
-            s = (s + hexp).reshape(16, 8, TB) + bias[None]
-            top = jnp.maximum(top, jnp.max(s, axis=0))
-            e_s[part, :] = s.reshape(128, TB)
-        top = jnp.max(top, axis=0, keepdims=True)
+        top = jnp.max(following, axis=0, keepdims=True)
+        following = lowest
         total = jnp.zeros((8, TB), F32)
         for w in range(groups):
             part = pl.ds(w * 128, 128)
-            e = jnp.exp2((e_s[part, :] - top) * EXPONENT)
+            e = jnp.exp2((e_s[tb % 2, part, :] - top) * EXPONENT)
             total = total + jnp.sum(e.reshape(16, 8, TB), axis=0)
-            e_s[part, :] = e
+            e_s[tb % 2, part, :] = e
+            if tb + 1 < blocks:
+                following = scores(tb + 1, w, following)
         inverse = 1.0 / jnp.sum(total, axis=0, keepdims=True)
         for w in range(groups):
             part = pl.ds(w * 128, 128)
-            p = e_s[part, :] * inverse
-            e_s[part, :] = p
+            p = e_s[tb % 2, part, :] * inverse
+            e_s[tb % 2, part, :] = p
             p_s[part, cols] = p.astype(BF16)
+        gt = gt_ref[0, :, cols]
         attended = dot(vt_s[pl.ds(rows, HD), :], p_s[:, cols])
         delta = jnp.sum(
             attended * gt_ref[0, pl.ds(own, HD), cols].astype(F32), axis=0, keepdims=True
@@ -245,7 +295,7 @@
         height = jnp.zeros((128, TB), F32)
         for w in range(groups):
             part = pl.ds(w * 128, 128)
-            d = e_s[part, :] * (dot(v_s[part, kwin], gt) - delta)
+            d = e_s[tb % 2, part, :] * (dot(v_s[part, kwin], gt) - delta)
             d_s[part, cols] = d.astype(BF16)
             height = height + d
             width = jnp.sum(d.reshape(16, 8, TB), axis=0)
@@ -341,7 +391,7 @@
             pltpu.VMEM((keys, C), BF16),
             pltpu.VMEM((C, keys), BF16),
             pltpu.VMEM((C, keys), BF16),
-            pltpu.VMEM((keys, TB), F32),
+            pltpu.VMEM((2, keys, TB), F32),
             pltpu.VMEM((keys, tokens), BF16),
             pltpu.VMEM((keys, tokens), BF16),
             pltpu.VMEM((keys, C), F32),
@@ -365,25 +415,73 @@
     )(at, mine, other, qt, gt, q, g, hexp, wexp, tht, twt)
 
 
+def table_kernel(at_ref, mine_ref, other_ref, height_ref, width_ref):
+    blocks, half, _ = mine_ref.shape
+
+    def fill(even, odd):
+        for w in range(blocks):
+            block = jnp.concatenate([even[w], odd[w]], 0).astype(F32)
+            first = 2 * half * w
+            count = min(2 * half, height_ref.shape[1] - first)
+            for i, out in enumerate((height_ref, width_ref)):
+                turned = block[:, 128 * i : 128 * (i + 1)].T
+                out[:, first : first + count] = turned[:HD, :count]
+
+    @pl.when(at_ref[2] == 0)
+    def _():
+        fill(mine_ref, other_ref)
+
+    @pl.when(at_ref[2] == 1)
+    def _():
+        fill(other_ref, mine_ref)
+
+
+def tables_out(at, mine, other, entries):
+    whole = pl.BlockSpec(memory_space=pltpu.VMEM)
+    height, width = pl.pallas_call(
+        table_kernel,
+        in_specs=[pl.BlockSpec(memory_space=pltpu.SMEM), whole, whole],
+        out_specs=[whole, whole],
+        out_shape=[jax.ShapeDtypeStruct((HD, entries), F32)] * 2,
+        name="tables",
+    )(at, mine, other)
+    return height.T, width.T
+
+
+def turn_kernel(dq_ref, out_ref):
+    for tb in range(dq_ref.shape[2] // TB):
+        block = dq_ref[:, :, pl.ds(tb * TB, TB)].reshape(C, TB).astype(F32).T.astype(BF16)
+        out_ref[:, pl.ds(tb * STRIDE, STRIDE), :] = block.reshape(-1, STRIDE, C)
+
+
+def turn(dq, shape):
+    whole = pl.BlockSpec(memory_space=pltpu.VMEM)
+    return pl.pallas_call(
+        turn_kernel,
+        in_specs=[whole],
+        out_specs=whole,
+        out_shape=jax.ShapeDtypeStruct(shape, BF16),
+        name="turn",
+    )(dq)
+
+
 def on_device(
     queries, key_tokens, value_tokens, out_grad, key_kernel, value_kernel, height_table, width_table
 ):
     own_rows, own_cols, _ = queries.shape
     rows_n, cols_n = lax.axis_size("ha"), lax.axis_size("wa")
-    tokens = own_rows * own_cols
     cells = own_cols // STRIDE
     ha, wa = lax.axis_index("ha"), lax.axis_index("wa")
     span = STRIDE * rows_n
 
-    part = jnp.stack([pool_partial(key_tokens, key_kernel), pool_partial(value_tokens, value_kernel)])
-    left = shift(part[:, :, cells], "wa", 1)
-    part = jnp.concatenate([part[:, :, :1] + left[:, :, None], part[:, :, 1:cells]], 2)
-    own = part[:, 0] + shift(part[:, 1], "ha", 1)
-    pooled = own.astype(BF16)
-    pooled, queries, out_grad, height_table, width_table = lax.optimization_barrier(
-        (pooled, queries, out_grad, height_table, width_table)
-    )
-    mine = jnp.broadcast_to(pooled[None], (rows_n // 2, 2, cells, C)).reshape(rows_n, cells, C)
+    own, down, right, corner = pool_partial(key_tokens, value_tokens, key_kernel, value_kernel)
+    corner = shift_both(corner, 1)
+    above = shift(down, "ha", 1)
+    left = shift(right, "wa", 1)
+    mine = pooled_copies(own, above, left, corner, rows_n)
+    mine, queries, out_grad, height_table, width_table = lax.optimization_barrier(
+        (mine, queries, out_grad, height_table, width_table)
+    )
     mine = exchange(mine, "ha").reshape(rows_n * cells, C)
     mine = to_all(mine, "wa").reshape(cols_n * rows_n * cells, C)
 
@@ -416,24 +514,17 @@
     table = sums[:, :, C:].astype(BF16).reshape(2, half, HD)
     table = jnp.pad(table, ((0, 0), (0, 0), (0, 128 - HD)))
     table = to_all(jnp.concatenate([table[0], table[1]], 1), "wa")
-    far = swap(table)
-    table = jnp.stack([jnp.where(ha % 2 == 0, table, far), jnp.where(ha % 2 == 0, far, table)], 1)
-    table = table.reshape(2 * span, 256)
-    height_grad = table[: height_table.shape[0], :HD].astype(F32)
-    width_grad = table[: width_table.shape[0], 128 : 128 + HD].astype(F32)
+    height_grad, width_grad = tables_out(at, table, swap(table), height_table.shape[0])
     sums = sums[:, :, :C]
 
+    corner = shift_both(sums[:, :1], -1)
+    below = shift(sums, "ha", -1)
     right = shift(sums[:, :1], "wa", -1)
-    below = shift(sums, "ha", -1)
-    corner = shift_both(sums[:, :1], -1)
-    cot = jnp.stack(
-        [jnp.concatenate([sums, right], 1), jnp.concatenate([below, corner], 1)], 1
-    )
-    key_grad = spread(cot[0], key_kernel)
-    value_grad = spread(cot[1], value_kernel)
-
-    query_grad = dq.reshape(C, cells, own_rows, STRIDE).transpose(2, 1, 3, 0)
-    query_grad = query_grad.reshape(own_rows, own_cols, C)
+    key_grad, value_grad = spread(
+        sums, right, below, corner, key_kernel, value_kernel, key_tokens.shape
+    )
+
+    query_grad = turn(dq, queries.shape)
     return (query_grad, key_grad, value_grad, height_grad, width_grad)
 
 

time: 164 us -> 164 us (level)
  the two profiles are of different devices: /device:TPU:2 before, /device:TPU:41 now
where the time goes in v1:
time: 164 us
  blocking collectives  47.6 us (29%)
  Pallas kernels  45.9 us (28%)
  starting transfers between devices  41.9 us (26%)
  waiting for transfers between devices  16.3 us (10%)
  local copies, waits for them, and re-layouts  7.43 us (5%)
  other arithmetic  3.45 us (2%)
    all_to_all x2, blocking collectives, exchange(): return lax.all_to_all(blocks, axis, 0, 0, tiled=False)  39.1 us
    pallas_call x1, Pallas kernels, attention(): pl.pallas_call(attention_kernel, grid=(HEADS,), in_specs=[pl.BlockSpec(me...  29.3 us
    ppermute x4, starting transfers between devices, shift(): lax.ppermute(block, axis, [(i, i + distance) for i in range(size) if 0 <=...  12.9 us
    all_to_all x1, starting transfers between devices, exchange(): return lax.all_to_all(blocks, axis, 0, 0, tiled=False)  10.1 us
    ppermute x2, starting transfers between devices, shift_both(): return lax.ppermute(block, ('ha', 'wa'), route)  9.77 us
    all_to_all x1, waiting for transfers between devices, exchange(): return lax.all_to_all(blocks, axis, 0, 0, tiled=False)  9.31 us
    all_to_all x1, blocking collectives, to_all(): return lax.all_to_all(copies, axis, 0, 0, tiled=False)  8.57 us
    pallas_call x1, Pallas kernels, prepare(): pl.pallas_call(prep_kernel, grid=(tokens // TB,), in_specs=[block, block,...  7.05 us
  transfers between devices with their start and end apart: 11, of which 4 were waited for; matrix products, arithmetic and copies ran while one was open for 2% of the time, Pallas kernels for 7%

profile of v1, /device:TPU:41, one launch (start us, length us, event | category | flops | bytes accessed | tf_op | source)
XLA Modules:
  0.0 163.5 jit_solution(7858764339377780673)
XLA Ops:
  0.6 1.7 %pool.1 = (f32[2,4,384]{2,1,0:T(4,128)}, f32[2,4,384]{2,1,0:T(4,128)}, f32[2,1,384]{2,1,0:T(1,128)}, f32[2,1,384]{2,1,0:T(1,128)}) custom-call(bf16[16,64,384]{2,1,0:T(8,128)(2,1)} %k15.1, bf16[16,64,384]{2,1,0:T(8,128)(2,1)} %k15.1, bf16[16,64,384]{2,1,0:T(8,128)(2,1)} %k15.1, bf16[16,64,384]{2,1,0:T(8,128)(2,1)} %v15.1, bf16[16,64,384]{2,1,0:T(8,128)(2,1)} %v15.1, ...), custom_call_target="tpu_custom_call" | custom-call | tf_op jit(solution)/shard_map/pool/pallas_call | solution.py:55
  2.3 5.3 %collective-permute-start = (f32[2,4,384]{2,1,0:T(4,128)}, f32[2,4,384]{2,1,0:T(4,128)S(1)}, u32[]{:S(2)}, u32[]{:S(2)}) collective-permute-start(f32[2,4,384]{2,1,0:T(4,128)} %get-tuple-element.33), channel_id=1, source_target_pairs={{0,8},{8,16},{16,24},{24,32},{32,40},{40,48},{48,56},{56,64},{64,7... | collective-permute-start | bytes 36872 | tf_op jit(solution)/shard_map/ppermute | solution.py:120
  7.7 2.2 %collective-permute-start.1 = (f32[2,1,384]{2,1,0:T(1,128)}, f32[2,1,384]{2,1,0:T(1,128)S(1)}, u32[]{:S(2)}, u32[]{:S(2)}) collective-permute-start(f32[2,1,384]{2,1,0:T(1,128)} %get-tuple-element.34), channel_id=1, source_target_pairs={{0,1},{1,2},{2,3},{3,4},{4,5},{5,6},{6,7},{8,9},{9,10},{10,11},{11... | collective-permute-start | bytes 9224 | tf_op jit(solution)/shard_map/ppermute | solution.py:120
  9.9 3.2 %collective-permute-start.2 = (f32[2,1,384]{2,1,0:T(1,128)}, f32[2,1,384]{2,1,0:T(1,128)S(1)}, u32[]{:S(2)}, u32[]{:S(2)}) collective-permute-start(f32[2,1,384]{2,1,0:T(1,128)} %get-tuple-element.35), channel_id=1, source_target_pairs={{0,9},{1,10},{2,11},{3,12},{4,13},{5,14},{6,15},{8,17},{9,18},{10,... | collective-permute-start | bytes 9224 | tf_op jit(solution)/shard_map/ppermute | solution.py:133
  13.1 0.0 collective-permute-done.1.left_ref
  13.1 3.1 %collective-permute-done.2.corner_ref = f32[2,1,384]{2,1,0:T(1,128)S(1)} collective-permute-done((f32[2,1,384]{2,1,0:T(1,128)}, f32[2,1,384]{2,1,0:T(1,128)S(1)}, u32[]{:S(2)}, u32[]{:S(2)}) %collective-permute-start.2) | collective-permute-done | bytes 3104 | tf_op jit(solution)/shard_map/ppermute | solution.py:133
  16.2 0.6 copy-done.11
  16.8 0.0 copy-done.7
  16.8 1.4 pooled.1
  18.2 10.1 %all-to-all-start = ((bf16[32,4,384]{2,1,0:T(4,128)(2,1)}), bf16[32,4,384]{2,1,0:T(4,128)(2,1)S(1)}, u32[]{:S(2)}, u32[]{:S(2)}) async-start(bf16[32,4,384]{2,1,0:T(4,128)(2,1)} %pooled.1), calls=%async_computation | async-start | bytes 196608 | tf_op jit(solution)/shard_map/all_to_all | solution.py:146
  28.3 9.3 %all-to-all-done = bf16[32,4,384]{2,1,0:T(4,128)(2,1)S(1)} async-done(((bf16[32,4,384]{2,1,0:T(4,128)(2,1)}), bf16[32,4,384]{2,1,0:T(4,128)(2,1)S(1)}, u32[]{:S(2)}, u32[]{:S(2)}) %all-to-all-start) | async-done | bytes 98336 | tf_op jit(solution)/shard_map/all_to_all | solution.py:146
  37.6 1.0 broadcast_in_dim.21
  38.6 4.4 %all-to-all-start.1 = ((bf16[8,128,384]{2,1,0:T(8,128)(2,1)}), bf16[8,128,384]{2,1,0:T(8,128)(2,1)S(1)}, u32[]{:S(2)}, u32[]{:S(2)}) async-start(bf16[8,128,384]{2,1,0:T(8,128)(2,1)} %broadcast_in_dim.21), calls=%async_computation.1 | async-start | bytes 1572864 | tf_op jit(solution)/shard_map/all_to_all | solution.py:142
  42.9 0.1 constant_dynamic-slice_fusion.1
  43.0 0.8 copy.19.th_ref
  43.8 0.1 constant_dynamic-slice_fusion
  43.9 0.8 copy.20.tw_ref
  44.7 0.7 fusion.2.tht_ref
  45.4 0.2 dynamic-slice_bitcast_fusion.3
  45.6 0.8 pad_maximum_fusion.1.twt_ref
  46.4 7.1 %prepare.1 = (bf16[4,256,1024]{2,1,0:T(8,128)(2,1)}, bf16[4,256,1024]{2,1,0:T(8,128)(2,1)}, f32[4,128,1024]{2,1,0:T(8,128)}, f32[4,64,1024]{2,1,0:T(8,128)}) custom-call(bf16[16,64,384]{2,1,0:T(8,128)(2,1)} %q_ref.1, bf16[16,64,384]{2,1,0:T(8,128)(2,1)} %g_ref.1, bf16[512,96]{1,0:T(8,128)(2,1)} %copy.19.th_ref, bf16[560,96]{1,0:T(8,128)(2,1)} %copy.20.tw_ref), custom_call_target="tpu_custom_call" | custom-call | flops 1610612736 | bytes 10485760 | tf_op jit(solution)/shard_map/prepare/pallas_call | solution.py:202
  53.5 1.5 collective-permute-start.3
  55.1 0.6 pad_add_fusion.at_ref
  55.6 1.4 collective-permute-done.3.other_ref
  57.0 0.9 copy-done.12
  57.9 29.3 %attention.1 = (bf16[1024,512]{1,0:T(8,128)(2,1)}, bf16[1024,512]{1,0:T(8,128)(2,1)}, bf16[4,96,1024]{2,1,0:T(8,128)(2,1)}) custom-call(s32[3]{0:T(128)} %pad_add_fusion.at_ref, bf16[1024,384]{1,0:T(8,128)(2,1)} %bitcast.36, bf16[1024,384]{1,0:T(8,128)(2,1)} %copy-done.12, bf16[4,256,1024]{2,1,0:T(8,128)(2,1)} %get-tuple-element.46.qt_ref, ...), custom_call_target="tpu_custom_call" | custom-call | flops 6442450944 | bytes 12582912 | tf_op jit(solution)/shard_map/attention/pallas_call | solution.py:367
  87.2 0.6 collective-permute-start.4
  87.8 2.5 %collective-permute-done.4 = bf16[1024,512]{1,0:T(8,128)(2,1)S(1)} collective-permute-done((bf16[1024,512]{1,0:T(8,128)(2,1)}, bf16[1024,512]{1,0:T(8,128)(2,1)S(1)}, u32[]{:S(2)}, u32[]{:S(2)}) %collective-permute-start.4) | collective-permute-done | bytes 1048608 | tf_op jit(solution)/shard_map/ppermute | solution.py:137
  90.3 1.5 add_convert_fusion
  91.8 17.7 %all_to_all.25 = bf16[8,128,512]{2,1,0:T(8,128)(2,1)S(1)} all-to-all(bf16[8,128,512]{2,1,0:T(8,128)(2,1)S(1)} %bitcast.32), channel_id=1, replica_groups=mesh['ha'=32,'wa'=8] {'wa'}, dimensions={0} | all-to-all | bytes 2097152 | tf_op jit(solution)/shard_map/all_to_all | solution.py:146
  109.5 0.1 reduce_sum.21
  109.7 0.1 broadcast_in_dim.22
  109.9 0.1 broadcast_in_dim.23
  110.0 0.2 pad_maximum_fusion
  110.2 21.4 %all_to_all.26 = bf16[32,4,1920]{2,1,0:T(4,128)(2,1)S(1)} all-to-all(bf16[32,4,1920]{2,1,0:T(4,128)(2,1)S(1)} %pad_maximum_fusion), channel_id=1, replica_groups=mesh['ha'=32,'wa'=8] {'ha'}, dimensions={0} | all-to-all | bytes 983040 | tf_op jit(solution)/shard_map/all_to_all | solution.py:146
  131.6 0.2 convert_reduce_fusion
  131.8 0.1 reshape.36
  131.9 8.6 %all_to_all.27.mine_ref = bf16[8,64,256]{2,1,0:T(8,128)(2,1)S(1)} all-to-all(bf16[8,64,256]{2,1,0:T(8,128)(2,1)S(1)} %broadcast_in_dim.24), channel_id=1, replica_groups=mesh['ha'=32,'wa'=8] {'wa'}, dimensions={0} | all-to-all | bytes 524288 | tf_op jit(solution)/shard_map/all_to_all | solution.py:142
  140.5 2.6 %collective-permute-start.8 = (bf16[8,64,256]{2,1,0:T(8,128)(2,1)S(1)}, bf16[8,64,256]{2,1,0:T(8,128)(2,1)S(1)}, u32[]{:S(2)}, u32[]{:S(2)}) collective-permute-start(bf16[8,64,256]{2,1,0:T(8,128)(2,1)S(1)} %all_to_all.27.mine_ref), channel_id=1, source_target_pairs={{0,8},{8,0},{16,24},{24,16},{32,40},{40,32},{48,56},{56,48},{64,72... | collective-permute-start | bytes 786440 | tf_op jit(solution)/shard_map/ppermute | solution.py:137
  143.2 1.9 %collective-permute-start.6 = (f32[2,4,384]{2,1,0:T(4,128)S(1)}, f32[2,4,384]{2,1,0:T(4,128)S(1)}, u32[]{:S(2)}, u32[]{:S(2)}) collective-permute-start(f32[2,4,384]{2,1,0:T(4,128)S(1)} %slice.49.sums_ref), channel_id=1, source_target_pairs={{8,0},{16,8},{24,16},{32,24},{40,32},{48,40},{56,48},{64,56},{72,6... | collective-permute-start | bytes 36872 | tf_op jit(solution)/shard_map/ppermute | solution.py:120
  145.1 6.6 %collective-permute-start.7 = (f32[2,1,384]{2,1,0:T(1,128)S(1)}, f32[2,1,384]{2,1,0:T(1,128)S(1)}, u32[]{:S(2)}, u32[]{:S(2)}) collective-permute-start(f32[2,1,384]{2,1,0:T(1,128)S(1)} %slice.50), channel_id=1, source_target_pairs={{9,0},{10,1},{11,2},{12,3},{13,4},{14,5},{15,6},{17,8},{18,9},{19,... | collective-permute-start | bytes 9224 | tf_op jit(solution)/shard_map/ppermute | solution.py:133
  151.7 3.4 %collective-permute-start.5 = (f32[2,1,384]{2,1,0:T(1,128)S(1)}, f32[2,1,384]{2,1,0:T(1,128)S(1)}, u32[]{:S(2)}, u32[]{:S(2)}) collective-permute-start(f32[2,1,384]{2,1,0:T(1,128)S(1)} %slice.50), channel_id=1, source_target_pairs={{1,0},{2,1},{3,2},{4,3},{5,4},{6,5},{7,6},{9,8},{10,9},{11,10},{12... | collective-permute-start | bytes 9224 | tf_op jit(solution)/shard_map/ppermute | solution.py:120
  155.1 2.3 %turn.1 = bf16[16,64,384]{2,1,0:T(8,128)(2,1)} custom-call(bf16[4,96,1024]{2,1,0:T(8,128)(2,1)} %get-tuple-element.52.dq_ref), custom_call_target="tpu_custom_call" | custom-call | tf_op jit(solution)/shard_map/turn/pallas_call | solution.py:459
  157.4 0.5 copy-done.8
  158.0 0.6 copy-done.6
  158.6 2.1 %spread.1 = (bf16[16,64,384]{2,1,0:T(8,128)(2,1)}, bf16[16,64,384]{2,1,0:T(8,128)(2,1)}) custom-call(f32[2,4,384]{2,1,0:T(4,128)} %copy-done.5, f32[2,1,384]{2,1,0:T(1,128)} %copy-done.9, f32[2,4,384]{2,1,0:T(4,128)} %copy-done.6, f32[2,1,384]{2,1,0:T(1,128)} %copy-done.8, bf16[3,3,384]{2,1,0:T(4,128)(2,1)} %kk_ref.3, bf16[3,3,384]{2,1,0:T(4,128)(2,1)} %vk_ref.3), custom_call_target="tpu_custom_call" | custom-call | tf_op jit(solution)/shard_map/spread/pallas_call | solution.py:109
  160.7 0.7 copy-done.4
  161.4 2.1 %tables.1 = (f32[96,1023]{1,0:T(8,128)}, f32[96,1023]{1,0:T(8,128)}) custom-call(s32[3]{0:T(128)} %pad_add_fusion.at_ref, bf16[8,64,256]{2,1,0:T(8,128)(2,1)} %copy-done.2, bf16[8,64,256]{2,1,0:T(8,128)(2,1)} %copy-done.4), custom_call_target="tpu_custom_call" | custom-call | tf_op jit(solution)/shard_map/tables/pallas_call | solution.py:441
  (36 shorter events, 0.2 us)
Async XLA Ops:
  0.6 42.3 %copy-start = (bf16[1023,96]{0,1:T(8,128)(2,1)S(1)}, bf16[1023,96]{0,1:T(8,128)(2,1)}, u32[]{:S(2)}) copy-start(bf16[1023,96]{0,1:T(8,128)(2,1)} %param.14) | copy-start | bytes 589252
  2.3 41.5 %copy-start.1 = (bf16[1023,96]{0,1:T(8,128)(2,1)S(1)}, bf16[1023,96]{0,1:T(8,128)(2,1)}, u32[]{:S(2)}) copy-start(bf16[1023,96]{0,1:T(8,128)(2,1)} %param.15) | copy-start | bytes 589252
  2.3 13.9 %collective-permute-start = (f32[2,4,384]{2,1,0:T(4,128)}, f32[2,4,384]{2,1,0:T(4,128)S(1)}, u32[]{:S(2)}, u32[]{:S(2)}) collective-permute-start(f32[2,4,384]{2,1,0:T(4,128)} %get-tuple-element.33), channel_id=1, source_target_pairs={{0,8},{8,16},{16,24},{24,32},{32,40},{40,48},{48,56},{56,64},{64,7... | collective-permute-start | bytes 36872 | tf_op jit(solution)/shard_map/ppermute | solution.py:120
  7.7 5.4 %collective-permute-start.1 = (f32[2,1,384]{2,1,0:T(1,128)}, f32[2,1,384]{2,1,0:T(1,128)S(1)}, u32[]{:S(2)}, u32[]{:S(2)}) collective-permute-start(f32[2,1,384]{2,1,0:T(1,128)} %get-tuple-element.34), channel_id=1, source_target_pairs={{0,1},{1,2},{2,3},{3,4},{4,5},{5,6},{6,7},{8,9},{9,10},{10,11},{11... | collective-permute-start | bytes 9224 | tf_op jit(solution)/shard_map/ppermute | solution.py:120
  9.9 6.3 %collective-permute-start.2 = (f32[2,1,384]{2,1,0:T(1,128)}, f32[2,1,384]{2,1,0:T(1,128)S(1)}, u32[]{:S(2)}, u32[]{:S(2)}) collective-permute-start(f32[2,1,384]{2,1,0:T(1,128)} %get-tuple-element.35), channel_id=1, source_target_pairs={{0,9},{1,10},{2,11},{3,12},{4,13},{5,14},{6,15},{8,17},{9,18},{10,... | collective-permute-start | bytes 9224 | tf_op jit(solution)/shard_map/ppermute | solution.py:133
  13.1 3.1 %copy-start.10 = (f32[2,1,384]{2,1,0:T(1,128)}, f32[2,1,384]{2,1,0:T(1,128)S(1)}, u32[]{:S(2)}) copy-start(f32[2,1,384]{2,1,0:T(1,128)S(1)} %collective-permute-done.1.left_ref) | copy-start | bytes 9220
  16.2 0.6 copy-start.11
  16.2 0.6 copy-start.7
  18.2 19.4 %all-to-all-start = ((bf16[32,4,384]{2,1,0:T(4,128)(2,1)}), bf16[32,4,384]{2,1,0:T(4,128)(2,1)S(1)}, u32[]{:S(2)}, u32[]{:S(2)}) async-start(bf16[32,4,384]{2,1,0:T(4,128)(2,1)} %pooled.1), calls=%async_computation | async-start | bytes 196608 | tf_op jit(solution)/shard_map/all_to_all | solution.py:146
  38.6 14.9 %all-to-all-start.1 = ((bf16[8,128,384]{2,1,0:T(8,128)(2,1)}), bf16[8,128,384]{2,1,0:T(8,128)(2,1)S(1)}, u32[]{:S(2)}, u32[]{:S(2)}) async-start(bf16[8,128,384]{2,1,0:T(8,128)(2,1)} %broadcast_in_dim.21), calls=%async_computation.1 | async-start | bytes 1572864 | tf_op jit(solution)/shard_map/all_to_all | solution.py:142
  53.5 3.5 %copy-start.3 = (bf16[8,128,384]{2,1,0:T(8,128)(2,1)}, bf16[8,128,384]{2,1,0:T(8,128)(2,1)S(1)}, u32[]{:S(2)}) copy-start(bf16[8,128,384]{2,1,0:T(8,128)(2,1)S(1)} %all-to-all-done.1) | copy-start | bytes 2359300
  53.5 3.5 %collective-permute-start.3 = (bf16[1024,384]{1,0:T(8,128)(2,1)S(1)}, bf16[1024,384]{1,0:T(8,128)(2,1)S(1)}, u32[]{:S(2)}, u32[]{:S(2)}) collective-permute-start(bf16[1024,384]{1,0:T(8,128)(2,1)S(1)} %bitcast.35), channel_id=1, source_target_pairs={{0,8},{8,0},{16,24},{24,16},{32,40},{40,32},{48,56},{56,48},{64,72... | collective-permute-start | bytes 2359304 | tf_op jit(solution)/shard_map/ppermute | solution.py:137
  57.0 0.9 copy-start.12
  87.2 3.1 %collective-permute-start.4 = (bf16[1024,512]{1,0:T(8,128)(2,1)}, bf16[1024,512]{1,0:T(8,128)(2,1)S(1)}, u32[]{:S(2)}, u32[]{:S(2)}) collective-permute-start(bf16[1024,512]{1,0:T(8,128)(2,1)} %get-tuple-element.54), channel_id=1, source_target_pairs={{0,8},{8,0},{16,24},{24,16},{32,40},{40,32},{48,56},{56,48},{64,72... | collective-permute-start | bytes 3145736 | tf_op jit(solution)/shard_map/ppermute | solution.py:137
  140.5 20.2 %copy-start.2 = (bf16[8,64,256]{2,1,0:T(8,128)(2,1)}, bf16[8,64,256]{2,1,0:T(8,128)(2,1)S(1)}, u32[]{:S(2)}) copy-start(bf16[8,64,256]{2,1,0:T(8,128)(2,1)S(1)} %all_to_all.27.mine_ref) | copy-start | bytes 786436
  140.5 20.2 %collective-permute-start.8 = (bf16[8,64,256]{2,1,0:T(8,128)(2,1)S(1)}, bf16[8,64,256]{2,1,0:T(8,128)(2,1)S(1)}, u32[]{:S(2)}, u32[]{:S(2)}) collective-permute-start(bf16[8,64,256]{2,1,0:T(8,128)(2,1)S(1)} %all_to_all.27.mine_ref), channel_id=1, source_target_pairs={{0,8},{8,0},{16,24},{24,16},{32,40},{40,32},{48,56},{56,48},{64,72... | collective-permute-start | bytes 786440 | tf_op jit(solution)/shard_map/ppermute | solution.py:137
  143.2 14.3 %copy-start.5 = (f32[2,4,384]{2,1,0:T(4,128)}, f32[2,4,384]{2,1,0:T(4,128)S(1)}, u32[]{:S(2)}) copy-start(f32[2,4,384]{2,1,0:T(4,128)S(1)} %slice.49.sums_ref) | copy-start | bytes 36868
  143.2 14.3 %collective-permute-start.6 = (f32[2,4,384]{2,1,0:T(4,128)S(1)}, f32[2,4,384]{2,1,0:T(4,128)S(1)}, u32[]{:S(2)}, u32[]{:S(2)}) collective-permute-start(f32[2,4,384]{2,1,0:T(4,128)S(1)} %slice.49.sums_ref), channel_id=1, source_target_pairs={{8,0},{16,8},{24,16},{32,24},{40,32},{48,40},{56,48},{64,56},{72,6... | collective-permute-start | bytes 36872 | tf_op jit(solution)/shard_map/ppermute | solution.py:120
  145.1 12.3 %collective-permute-start.7 = (f32[2,1,384]{2,1,0:T(1,128)S(1)}, f32[2,1,384]{2,1,0:T(1,128)S(1)}, u32[]{:S(2)}, u32[]{:S(2)}) collective-permute-start(f32[2,1,384]{2,1,0:T(1,128)S(1)} %slice.50), channel_id=1, source_target_pairs={{9,0},{10,1},{11,2},{12,3},{13,4},{14,5},{15,6},{17,8},{18,9},{19,... | collective-permute-start | bytes 9224 | tf_op jit(solution)/shard_map/ppermute | solution.py:133
  151.7 5.7 %collective-permute-start.5 = (f32[2,1,384]{2,1,0:T(1,128)S(1)}, f32[2,1,384]{2,1,0:T(1,128)S(1)}, u32[]{:S(2)}, u32[]{:S(2)}) collective-permute-start(f32[2,1,384]{2,1,0:T(1,128)S(1)} %slice.50), channel_id=1, source_target_pairs={{1,0},{2,1},{3,2},{4,3},{5,4},{6,5},{7,6},{9,8},{10,9},{11,10},{12... | collective-permute-start | bytes 9224 | tf_op jit(solution)/shard_map/ppermute | solution.py:120
  157.4 0.6 copy-start.8
  157.4 0.6 copy-start.9
  158.0 0.6 copy-start.6
  160.7 0.7 copy-start.4
